TPU v7x, 128 devices: a whole 4x4x4 slice. The times are simulated.
128 devices in a mesh: row: 8 (over z_hi, y), col: 16 (over z_lo, x, core).
Axes of the slice: x: 4, y: 4, z: 4 (z_hi: 2, z_lo: 2; z = z_hi * 2 + z_lo), core: 2. Of those that a mesh axis runs over, the one named last changes fastest.
Arguments:
- features: bfloat16 [65536, 256], P(('col', 'row')), may hold values from -6 to 6
- weight: bfloat16 [256, 256], replicated, may hold values from -0.375 to 0.375
- bias: float32 [256], replicated, may hold values from -4 to 4
- cotangent: bfloat16 [65536, 256], P(('row', 'col')), may hold values from -6 to 6
- tiles: bfloat16 [8, 16, 384, 128, 128], P('row', 'col'), may hold values from -0.0546875 to 0.0546875
- tile_rows: int32 [8, 16, 384], P('row', 'col'), may hold values from 0 to 63, as said below
- tile_cols: int32 [8, 16, 384], P('row', 'col'), may hold values from 0 to 31
- tile_counts: int32 [8, 16], P('row', 'col'), may hold values from 24 to 384, as said below
Outputs:
- hidden: bfloat16 [65536, 256], P(('row', 'col'))
- grad_weight: float32 [256, 256], replicated
- grad_bias: float32 [256], replicated
- grad_features: bfloat16 [65536, 256], P(('col', 'row'))
Inputs may be any that keep to these rules, and one draw needn't show every extreme that they name: `tile_rows`: on each grid cell the slots name distinct blocks. `tile_counts`: slots at or after a cell's count are unused; some cell uses all 384 slots.
All inputs are finite; a program needn't handle non-finite values.
Results may differ from a plain program's by a relative error of at most 0.013.
Values may be sent and summed in bfloat16 or wider, within the bound.
A program may use at most 128 MiB of HBM per device.

v0:
```python
import math
import jax
import jax.numpy as jnp
from jax import lax
from jax.sharding import PartitionSpec as P


def accumulate(tiles, dest_ids, source_ids, live_count, source_blocks, out_blocks, backward):
    slots = tiles.shape[0]
    group = math.gcd(slots, 32)
    block = tiles.shape[-1]
    width = source_blocks.shape[-1]
    in_blocks = source_blocks.shape[0]
    flat_source = source_blocks.reshape(in_blocks, block * width)
    in_range = jnp.arange(in_blocks, dtype=jnp.int32)
    out_range = jnp.arange(out_blocks, dtype=jnp.int32)

    def one_group(step_index, total):
        start = step_index * group
        tile_group = lax.dynamic_slice_in_dim(tiles, start, group, 0)
        dest_group = lax.dynamic_slice_in_dim(dest_ids, start, group, 0)
        source_group = lax.dynamic_slice_in_dim(source_ids, start, group, 0)
        live = start + jnp.arange(group, dtype=jnp.int32) < live_count
        if backward:
            fetch_ids = dest_group
            target = source_group
        else:
            fetch_ids = source_group
            target = dest_group
        picker = (fetch_ids[:, None] == in_range[None, :]).astype(jnp.bfloat16)
        fetched = jnp.dot(picker, flat_source, preferred_element_type=jnp.float32)
        fetched = fetched.astype(jnp.bfloat16).reshape(group, block, width)
        if backward:
            contrib = jnp.einsum(
                "tji,tjf->tif", tile_group, fetched, preferred_element_type=jnp.float32
            )
        else:
            contrib = jnp.einsum(
                "tij,tjf->tif", tile_group, fetched, preferred_element_type=jnp.float32
            )
        placer = ((target[:, None] == out_range[None, :]) & live[:, None]).astype(jnp.float32)
        added = jnp.dot(
            placer.T,
            contrib.reshape(group, block * width),
            precision=lax.Precision.HIGHEST,
            preferred_element_type=jnp.float32,
        )
        return total + added

    start_total = jnp.zeros((out_blocks, block * width), jnp.float32)
    result = lax.fori_loop(0, slots // group, one_group, start_total)
    return result.reshape(out_blocks, block, width)


def per_device(features, weight, bias, cotangent, tiles, tile_rows, tile_cols, tile_counts):
    tile_set = tiles[0, 0]
    dest_ids = tile_rows[0, 0]
    source_ids = tile_cols[0, 0]
    live_count = tile_counts[0, 0]
    block = tile_set.shape[-1]
    own_nodes = features.shape[0]
    width = features.shape[1]
    row_count = lax.axis_size("row")
    col_count = lax.axis_size("col")
    blocks_down = own_nodes * col_count // block
    blocks_across = own_nodes * row_count // block
    factor = 1.0 / math.sqrt(own_nodes * row_count * col_count)
    panel = lax.all_gather(features, "row", axis=0, tiled=True)
    panel_blocks = panel.reshape(blocks_across, block, width)
    partial_value = accumulate(
        tile_set, dest_ids, source_ids, live_count, panel_blocks, blocks_down, False
    )
    term = partial_value.reshape(blocks_down * block, width)
    summed = lax.psum_scatter(term, "col", scatter_dimension=0, tiled=True)
    aggregated = summed.astype(jnp.bfloat16)
    preact = jnp.dot(aggregated, weight, preferred_element_type=jnp.float32) + bias
    hidden = jax.nn.silu(preact).astype(jnp.bfloat16)
    sigma = jax.nn.sigmoid(preact)
    slope = sigma * (1.0 + preact * (1.0 - sigma))
    grad_pre = (cotangent.astype(jnp.float32) * slope).astype(jnp.bfloat16)
    local_weight = jnp.einsum("nf,ng->fg", aggregated, grad_pre, preferred_element_type=jnp.float32)
    local_bias = jnp.sum(grad_pre.astype(jnp.float32), axis=0)
    grad_agg = jnp.dot(grad_pre, weight.T, preferred_element_type=jnp.float32).astype(jnp.bfloat16)
    grad_panel = lax.all_gather(grad_agg, "col", axis=0, tiled=True)
    grad_blocks = grad_panel.reshape(blocks_down, block, width)
    partial_back = accumulate(
        tile_set, dest_ids, source_ids, live_count, grad_blocks, blocks_across, True
    )
    term_back = partial_back.reshape(blocks_across * block, width)
    grad_features = lax.psum_scatter(
        term_back.astype(jnp.bfloat16), "row", scatter_dimension=0, tiled=True
    )
    grad_weight, grad_bias = lax.psum((local_weight, local_bias), ("row", "col"))
    grad_weight = grad_weight * factor
    grad_bias = grad_bias * factor
    return (hidden, grad_weight, grad_bias, grad_features)


def solution(mesh):
    in_specs = (
        P(("col", "row"), None),
        P(),
        P(),
        P(("row", "col"), None),
        P("row", "col", None, None, None),
        P("row", "col", None),
        P("row", "col", None),
        P("row", "col"),
    )
    out_specs = (P(("row", "col"), None), P(), P(), P(("col", "row"), None))
    return jax.shard_map(
        per_device, mesh=mesh, in_specs=in_specs, out_specs=out_specs, check_vma=False
    )
```

profile of v0, /device:TPU:0, one launch (start us, length us, event | category | flops | bytes accessed | tf_op | source)
XLA Modules:
  0.0 667.1 jit_solution(5247763881698745133)
XLA Ops:
  9.4 58.5 %all-gather.3.cloned.1.call-done = bf16[4096,256]{1,0:T(8,128)(2,1)} async-done(((bf16[512,256]{1,0:T(8,128)(2,1)}), bf16[4096,256]{1,0:T(8,128)(2,1)}) %all-gather.3.cloned.1.call-update) | async-done | bytes 2097168 | tf_op jit(solution)/shard_map/all_gather | solution.py:68
  70.7 196.6 %while.28 = (s32[]{:T(128)}, f32[64,32768]{1,0:T(8,128)}, s32[384]{0:T(512)S(1)}, s32[]{:T(128)}, bf16[384,128,128]{2,1,0:T(8,128)(2,1)}, /*index=5*/s32[384]{0:...) while((s32[]{:T(128)}, f32[64,32768]{1,0:T(8,128)}, ...), condition=%wide.region_1.0_spmd.clone, body=%wide.region_0.0_spmd.clone.sunk | while | flops 1146098688 | bytes 103810120 | solution.py:51
  77.4 6.5 convolution_add_fusion.5
  93.8 6.5 convolution_add_fusion.5
  110.1 6.5 convolution_add_fusion.5
  126.5 6.5 convolution_add_fusion.5
  142.9 6.5 convolution_add_fusion.5
  159.3 6.5 convolution_add_fusion.5
  175.7 6.5 convolution_add_fusion.5
  192.0 6.5 convolution_add_fusion.5
  208.4 6.5 convolution_add_fusion.5
  224.8 6.5 convolution_add_fusion.5
  241.2 6.5 convolution_add_fusion.5
  257.6 6.5 convolution_add_fusion.5
  267.3 9.2 %reshape_reshape.11 = f32[8192,256]{1,0:T(8,128)} reshape(f32[64,32768]{1,0:T(8,128)} %get-tuple-element.312) | data formatting | bytes 16777216 | tf_op jit(solution)/shard_map/reshape;reshape | solution.py:73
  276.6 73.4 %reduce-scatter.3.cloned.1.call-done = f32[512,256]{1,0:T(8,128)} async-done(((f32[8192,256]{1,0:T(8,128)}), f32[512,256]{1,0:T(8,128)}) %reduce-scatter.3.cloned.1.call-update) | async-done | bytes 524304 | tf_op jit(solution)/shard_map/reduce_scatter | solution.py:74
  353.4 16.7 %copy.12 = bf16[1,1,384,128,128]{3,4,2,1,0:T(8,128)(2,1)} copy(bf16[1,1,384,128,128]{4,3,2,1,0:T(8,128)(2,1)} %bitcast.60) | data formatting | bytes 25165824 | tf_op args[4]
  371.2 18.1 %all-gather.5.cloned.1.call-done = bf16[8192,256]{1,0:T(8,128)(2,1)} async-done(((bf16[512,256]{1,0:T(8,128)(2,1)}), bf16[8192,256]{1,0:T(8,128)(2,1)}) %all-gather.5.cloned.1.call-update) | async-done | bytes 4194320 | tf_op jit(solution)/shard_map/all_gather | solution.py:84
  389.2 7.4 %reshape_reshape.12 = bf16[64,32768]{1,0:T(8,128)(2,1)} reshape(bf16[8192,256]{1,0:T(8,128)(2,1)} %all-gather.5.cloned.1.call-done) | data formatting | bytes 8388608 | tf_op jit(solution)/shard_map/reshape;reshape | solution.py:14
  396.6 183.3 %while.29 = (s32[]{:T(128)}, f32[32,32768]{1,0:T(8,128)}, s32[384]{0:T(512)S(1)}, s32[]{:T(128)}, bf16[384,128,128]{1,2,0:T(8,128)(2,1)}, /*index=5*/s32[384]{0:...) while((s32[]{:T(128)}, f32[32,32768]{1,0:T(8,128)}, ...), condition=%wide.region_7.8_spmd.clone, body=%wide.region_6.7_spmd.clone.sunk | while | flops 808456256 | bytes 72352824 | solution.py:51
  481.7 4.7 convolution_add_fusion.6
  496.9 4.7 convolution_add_fusion.6
  573.3 4.7 convolution_add_fusion.6
  584.7 69.3 %psum.15 = f32[256]{0:T(256)S(1)} all-reduce(f32[256]{0:T(256)S(1)} %get-tuple-element.405), channel_id=1, replica_groups=mesh['row'=8,'col'=16] {'row','col'}, use_global_device_ids=true, to_apply=%region_5.6 | all-reduce | flops 256 | bytes 2048 | tf_op jit(solution)/shard_map/psum | solution.py:93
  (343 shorter events, 306.8 us)
Async XLA Ops:
  7.2 342.9 %copy-start = (bf16[256,256]{1,0:T(8,128)(2,1)S(1)}, bf16[256,256]{1,0:T(8,128)(2,1)}, u32[]{:S(2)}) copy-start(bf16[256,256]{1,0:T(8,128)(2,1)} %param.13) | copy-start | bytes 393220
  7.2 60.7 %all-gather.3.cloned.1.call-start = ((), (), s32[]{:S(2)}) async-start(), calls=%async_computation.2 | async-start | bytes 2359296 | tf_op jit(solution)/shard_map/all_gather | solution.py:68
  7.9 342.1 %reduce-scatter.3.cloned.1.call-start = ((), (), s32[]{:S(2)}) async-start(), calls=%async_computation.3 | async-start | bytes 8912896 | tf_op jit(solution)/shard_map/reduce_scatter | solution.py:74
  72.8 4.5 slice-start
  89.2 4.5 slice-start
  100.3 3.2 copy-start.2
  105.6 4.5 slice-start
  116.7 3.2 copy-start.2
  122.0 4.5 slice-start
  138.3 4.5 slice-start
  154.7 4.5 slice-start
  171.1 4.5 slice-start
  187.5 4.5 slice-start
  203.8 4.5 slice-start
  220.2 4.5 slice-start
  236.6 4.5 slice-start
  253.0 4.5 slice-start
  276.6 73.5 %copy-start.6 = (bf16[512,256]{1,0:T(8,128)(2,1)S(1)}, bf16[512,256]{1,0:T(8,128)(2,1)}, u32[]{:S(2)}) copy-start(bf16[512,256]{1,0:T(8,128)(2,1)} %param.15) | copy-start | bytes 786436
  276.6 73.5 %copy-start.7 = (f32[256]{0:T(256)S(1)}, f32[256]{0:T(256)}, u32[]{:S(2)}) copy-start(f32[256]{0:T(256)} %param.14) | copy-start | bytes 3076
  276.6 112.7 %all-gather.5.cloned.1.call-start = ((), (), s32[]{:S(2)}) async-start(), calls=%async_computation.5 | async-start | bytes 4456448 | tf_op jit(solution)/shard_map/all_gather | solution.py:84
  353.2 301.4 %all-reduce.2.cloned.1.call-start = ((), (), s32[]{:S(2)}) async-start(), calls=%async_computation.4 | async-start | bytes 524288 | tf_op jit(solution)/shard_map/psum | solution.py:93
  353.4 16.7 %copy-start.5 = (f32[512,256]{1,0:T(8,128)S(1)}, f32[512,256]{1,0:T(8,128)}, u32[]{:S(2)}) copy-start(f32[512,256]{1,0:T(8,128)} %reduce-scatter.3.cloned.1.call-done) | copy-start | bytes 1572868
  371.1 289.5 %reduce-scatter.5.cloned.1.call-start = ((), (), s32[]{:S(2)}) async-start(), calls=%async_computation.6 | async-start | bytes 2359296 | tf_op jit(solution)/shard_map/reduce_scatter | solution.py:90
  579.9 80.7 %copy-start.1 = (bf16[256,256]{1,0:T(8,128)(2,1)S(1)}, bf16[256,256]{1,0:T(8,128)(2,1)}, u32[]{:S(2)}) copy-start(bf16[256,256]{1,0:T(8,128)(2,1)} %param.13) | copy-start | bytes 393220
  (46 other events, 114.6 us)
Sparse Core Ops, SparseCore 0:
  10.4 57.4 all-gather.2
  276.7 73.2 reduce-scatter.2
  353.3 35.9 all-gather.4
  394.4 141.9 all-reduce.1
  584.8 75.7 reduce-scatter.4
where the time goes:
time: 669 us; the launch traced here: 667 us
  matrix products  231 us (35%)
  local copies, waits for them, and re-layouts  174 us (26%)
  waiting for transfers between devices  155 us (23%)
  blocking collectives  69.3 us (10%)
  other arithmetic  21.7 us (3%)
  between operations  13.8 us (2%)
    dot_general x24, matrix products, one_group(): jnp.dot(placer.T, contrib.reshape(group, block * width), precision=lax.Pr...  134 us
    while x168, local copies, waits for them, and re-layouts  132 us
    reduce_scatter x1, waiting for transfers between devices, per_device(): summed = lax.psum_scatter(term, 'col', scatter_dimension=0, tiled=True)  73.4 us
    psum x1, blocking collectives, per_device(): lax.psum((local_weight, local_bias), ('row', 'col'))  69.3 us
    all_gather x1, waiting for transfers between devices, per_device(): panel = lax.all_gather(features, 'row', axis=0, tiled=True)  58.5 us
    dot_general x24, matrix products, one_group(): fetched = jnp.dot(picker, flat_source, preferred_element_type=jnp.float32)  44.3 us
    dot_general x12, matrix products, one_group(): jnp.einsum('tij,tjf->tif', tile_group, fetched, preferred_element_type=jn...  25 us
    dot_general x12, matrix products, one_group(): jnp.einsum('tji,tjf->tif', tile_group, fetched, preferred_element_type=jn...  23.2 us
  transfers between devices with their start and end apart: 5, of which 4 were waited for; matrix products, arithmetic and copies ran while one was open for 29% of the time, Pallas kernels for 0%

commit v1 on v0

--- a/solution.py
+++ b/solution.py
@@ -53,6 +53,11 @@
 
 
 def per_device(features, weight, bias, cotangent, tiles, tile_rows, tile_cols, tile_counts):
+
+    def supply_field(own_rows):
+        block_last = jax.lax.psum(own_rows, axis_name="col")
+        return jax.lax.psum(block_last, axis_name="row")
+
     tile_set = tiles[0, 0]
     dest_ids = tile_rows[0, 0]
     source_ids = tile_cols[0, 0]
@@ -90,7 +95,7 @@
     grad_features = lax.psum_scatter(
         term_back.astype(jnp.bfloat16), "row", scatter_dimension=0, tiled=True
     )
-    grad_weight, grad_bias = lax.psum((local_weight, local_bias), ("row", "col"))
+    grad_weight, grad_bias = supply_field((local_weight, local_bias))
     grad_weight = grad_weight * factor
     grad_bias = grad_bias * factor
     return (hidden, grad_weight, grad_bias, grad_features)

time: 669 us -> 790 us (1.18)
  waiting for transfers between devices: 155 us -> 291 us
  blocking collectives: 69.3 us -> 53.6 us
    psum x1 -> x2, waiting for transfers between devices: 0.01 us -> 97.3 us  [the longest x1 97.3 us: supply_field(): block_last = jax.lax.psum(own_rows, axis_name='col')]
    all_gather x1, waiting for transfers between devices: 18.1 us -> 40.8 us  [per_device(): grad_panel = lax.all_gather(grad_agg, 'col', axis=0, tiled=True)]
    psum x1 -> x2, blocking collectives: 69.3 us -> 53.6 us  [the longest x1 29.3 us: supply_field(): block_last = jax.lax.psum(own_rows, axis_name='col')]
    reduce_scatter x1, waiting for transfers between devices: 4.32 us -> 19.9 us  [per_device(): lax.psum_scatter(term_back.astype(jnp.bfloat16), 'row', scatter_dimension...]
    unnamed x11 -> x9, local copies, waits for them, and re-layouts: 16.7 us -> 16.7 us
  transfers between devices with their start and end apart: 5 -> 6, of which waited for: 4 -> 5; matrix products, arithmetic and copies ran while one was open for 29% -> 24% of each run, Pallas kernels for 0% -> 0%
where the time goes in v1:
time: 790 us; the launch traced here: 788 us
  waiting for transfers between devices  291 us (37%)
  matrix products  232 us (29%)
  local copies, waits for them, and re-layouts  174 us (22%)
  blocking collectives  53.6 us (7%)
  other arithmetic  21.7 us (3%)
  between operations  14.2 us (2%)
    dot_general x24, matrix products, one_group(): jnp.dot(placer.T, contrib.reshape(group, block * width), precision=lax.Pr...  134 us
    while x168, local copies, waits for them, and re-layouts  132 us
    psum x1, waiting for transfers between devices, supply_field(): block_last = jax.lax.psum(own_rows, axis_name='col')  97.3 us
    reduce_scatter x1, waiting for transfers between devices, per_device(): summed = lax.psum_scatter(term, 'col', scatter_dimension=0, tiled=True)  73.4 us
    all_gather x1, waiting for transfers between devices, per_device(): panel = lax.all_gather(features, 'row', axis=0, tiled=True)  58.5 us
    dot_general x24, matrix products, one_group(): fetched = jnp.dot(picker, flat_source, preferred_element_type=jnp.float32)  44.3 us
    all_gather x1, waiting for transfers between devices, per_device(): grad_panel = lax.all_gather(grad_agg, 'col', axis=0, tiled=True)  40.8 us
    psum x1, blocking collectives, supply_field(): block_last = jax.lax.psum(own_rows, axis_name='col')  29.3 us
  transfers between devices with their start and end apart: 6, of which 5 were waited for; matrix products, arithmetic and copies ran while one was open for 24% of the time, Pallas kernels for 0%

profile of v1, /device:TPU:0, one launch (start us, length us, event | category | flops | bytes accessed | tf_op | source)
XLA Modules:
  0.0 788.1 jit_solution(10056470270507905791)
XLA Ops:
  9.4 58.5 %all-gather.3.cloned.1.call-done = bf16[4096,256]{1,0:T(8,128)(2,1)} async-done(((bf16[512,256]{1,0:T(8,128)(2,1)}), bf16[4096,256]{1,0:T(8,128)(2,1)}) %all-gather.3.cloned.1.call-update) | async-done | bytes 2097168 | tf_op jit(solution)/shard_map/all_gather | solution.py:73
  70.7 196.6 %while.28 = (s32[]{:T(128)}, f32[64,32768]{1,0:T(8,128)}, s32[384]{0:T(512)S(1)}, s32[]{:T(128)}, bf16[384,128,128]{2,1,0:T(8,128)(2,1)}, /*index=5*/s32[384]{0:...) while((s32[]{:T(128)}, f32[64,32768]{1,0:T(8,128)}, ...), condition=%wide.region_1.0_spmd.clone, body=%wide.region_0.0_spmd.clone.sunk | while | flops 1146098688 | bytes 103810120 | solution.py:51
  77.4 6.5 convolution_add_fusion.5
  93.8 6.5 convolution_add_fusion.5
  110.2 6.5 convolution_add_fusion.5
  126.5 6.5 convolution_add_fusion.5
  142.9 6.5 convolution_add_fusion.5
  159.3 6.5 convolution_add_fusion.5
  175.7 6.5 convolution_add_fusion.5
  192.1 6.5 convolution_add_fusion.5
  208.4 6.5 convolution_add_fusion.5
  224.8 6.5 convolution_add_fusion.5
  241.2 6.5 convolution_add_fusion.5
  257.6 6.5 convolution_add_fusion.5
  267.3 9.3 %reshape_reshape.11 = f32[8192,256]{1,0:T(8,128)} reshape(f32[64,32768]{1,0:T(8,128)} %get-tuple-element.312) | data formatting | bytes 16777216 | tf_op jit(solution)/shard_map/reshape;reshape | solution.py:78
  276.7 73.4 %reduce-scatter.3.cloned.1.call-done = f32[512,256]{1,0:T(8,128)} async-done(((f32[8192,256]{1,0:T(8,128)}), f32[512,256]{1,0:T(8,128)}) %reduce-scatter.3.cloned.1.call-update) | async-done | bytes 524304 | tf_op jit(solution)/shard_map/reduce_scatter | solution.py:79
  355.5 16.6 %copy.12 = bf16[1,1,384,128,128]{3,4,2,1,0:T(8,128)(2,1)} copy(bf16[1,1,384,128,128]{4,3,2,1,0:T(8,128)(2,1)} %bitcast.60) | data formatting | bytes 25165824 | tf_op args[4]
  372.2 97.3 %all-reduce.3.cloned.1.call-done = f32[256,256]{1,0:T(8,128)} async-done(((f32[256,256]{1,0:T(8,128)}), f32[256,256]{1,0:T(8,128)}) %all-reduce.3.cloned.1.call-update) | async-done | bytes 262160 | tf_op jit(solution)/shard_map/psum | solution.py:58
  469.5 40.8 %all-gather.5.cloned.1.call-done = bf16[8192,256]{1,0:T(8,128)(2,1)} async-done(((bf16[512,256]{1,0:T(8,128)(2,1)}), bf16[8192,256]{1,0:T(8,128)(2,1)}) %all-gather.5.cloned.1.call-update) | async-done | bytes 4194320 | tf_op jit(solution)/shard_map/all_gather | solution.py:89
  510.3 7.4 reshape_reshape.12
  517.7 183.0 %while.29 = (s32[]{:T(128)}, f32[32,32768]{1,0:T(8,128)}, s32[384]{0:T(512)S(1)}, s32[]{:T(128)}, bf16[384,128,128]{1,2,0:T(8,128)(2,1)}, /*index=5*/s32[384]{0:...) while((s32[]{:T(128)}, f32[32,32768]{1,0:T(8,128)}, ...), condition=%wide.region_9.10_spmd.clone, body=%wide.region_8.9_spmd.clone.sunk | while | flops 808456256 | bytes 72352824 | solution.py:51
  705.5 29.3 %psum.30 = f32[256]{0:T(256)S(1)} all-reduce(f32[256]{0:T(256)S(1)} %get-tuple-element.405), channel_id=1, replica_groups=mesh['row'=8,'col'=16] {'col'}, use_global_device_ids=true, to_apply=%region_6.7 | all-reduce | flops 256 | bytes 2048 | tf_op jit(solution)/shard_map/psum | solution.py:58
  734.9 24.3 %psum.31 = f32[256]{0:T(256)S(1)} all-reduce(f32[256]{0:T(256)S(1)} %psum.30), channel_id=1, replica_groups=mesh['row'=8,'col'=16] {'row'}, use_global_device_ids=true, to_apply=%region_7.8 | all-reduce | flops 256 | bytes 2048 | tf_op jit(solution)/shard_map/psum | solution.py:59
  761.4 19.9 %reduce-scatter.5.cloned.1.call-done = bf16[512,256]{1,0:T(8,128)(2,1)} async-done(((bf16[4096,256]{1,0:T(8,128)(2,1)}), bf16[512,256]{1,0:T(8,128)(2,1)}) %reduce-scatter.5.cloned.1.call-update) | async-done | bytes 262160 | tf_op jit(solution)/shard_map/reduce_scatter | solution.py:95
  (345 shorter events, 317.3 us)
Async XLA Ops:
  7.2 342.9 %copy-start = (bf16[256,256]{1,0:T(8,128)(2,1)S(1)}, bf16[256,256]{1,0:T(8,128)(2,1)}, u32[]{:S(2)}) copy-start(bf16[256,256]{1,0:T(8,128)(2,1)} %param.13) | copy-start | bytes 393220
  7.2 60.7 %all-gather.3.cloned.1.call-start = ((), (), s32[]{:S(2)}) async-start(), calls=%async_computation.2 | async-start | bytes 2359296 | tf_op jit(solution)/shard_map/all_gather | solution.py:73
  7.9 342.1 %reduce-scatter.3.cloned.1.call-start = ((), (), s32[]{:S(2)}) async-start(), calls=%async_computation.3 | async-start | bytes 8912896 | tf_op jit(solution)/shard_map/reduce_scatter | solution.py:79
  72.8 4.5 slice-start
  89.2 4.5 slice-start
  100.3 3.2 copy-start.2
  105.6 4.5 slice-start
  116.7 3.2 copy-start.2
  122.0 4.5 slice-start
  138.3 4.5 slice-start
  154.7 4.5 slice-start
  171.1 4.5 slice-start
  187.5 4.5 slice-start
  203.9 4.5 slice-start
  220.2 4.5 slice-start
  236.6 4.5 slice-start
  253.0 4.5 slice-start
  276.6 73.5 %copy-start.5 = (bf16[512,256]{1,0:T(8,128)(2,1)S(1)}, bf16[512,256]{1,0:T(8,128)(2,1)}, u32[]{:S(2)}) copy-start(bf16[512,256]{1,0:T(8,128)(2,1)} %param.15) | copy-start | bytes 786436
  276.6 73.5 %copy-start.6 = (f32[256]{0:T(256)S(1)}, f32[256]{0:T(256)}, u32[]{:S(2)}) copy-start(f32[256]{0:T(256)} %param.14) | copy-start | bytes 3076
  276.6 192.8 %all-reduce.3.cloned.1.call-start = ((), (), s32[]{:S(2)}) async-start(), calls=%async_computation.4 | async-start | bytes 524288 | tf_op jit(solution)/shard_map/psum | solution.py:58
  354.2 156.0 %all-gather.5.cloned.1.call-start = ((), (), s32[]{:S(2)}) async-start(), calls=%async_computation.6 | async-start | bytes 4456448 | tf_op jit(solution)/shard_map/all_gather | solution.py:89
  355.3 404.4 %all-reduce.5.cloned.1.call-start = ((), (), s32[]{:S(2)}) async-start(), calls=%async_computation.5 | async-start | bytes 524288 | tf_op jit(solution)/shard_map/psum | solution.py:59
  469.4 311.8 %reduce-scatter.5.cloned.1.call-start = ((), (), s32[]{:S(2)}) async-start(), calls=%async_computation.7 | async-start | bytes 2359296 | tf_op jit(solution)/shard_map/reduce_scatter | solution.py:95
  700.7 80.5 %copy-start.1 = (bf16[256,256]{1,0:T(8,128)(2,1)S(1)}, bf16[256,256]{1,0:T(8,128)(2,1)}, u32[]{:S(2)}) copy-start(bf16[256,256]{1,0:T(8,128)(2,1)} %param.13) | copy-start | bytes 393220
  (46 other events, 114.4 us)
Sparse Core Ops, SparseCore 0:
  10.4 57.4 all-gather.2
  276.7 73.2 reduce-scatter.2
  354.4 115.0 all-reduce.2
  471.7 38.5 all-gather.4
  512.7 84.6 all-reduce.4
  705.6 75.5 reduce-scatter.4
